TPU v7x, 256 devices: a whole 4x4x8 slice. The times are simulated.
256 devices in a mesh: dp: 4 (over y), brick: 64 (over z, x, core).
Axes of the slice: x: 4, y: 4, z: 8, core: 2. Of those that a mesh axis runs over, the one named last changes fastest.
Arguments:
- features: bfloat16 [4, 512, 512, 64], P('dp', 'brick'), may hold values from -6 to 6
- occupancy: int32 [4, 512, 512], P('dp', 'brick'), may hold values 0 or 1
- neighbours: int32 [4, 512, 27], P('dp', 'brick'), may hold values from -1 to 511, as said below
- owners: int32 [4, 512], P('dp', 'brick'), may hold values from 0 to 511, as said below
- w_conv: bfloat16 [3, 3, 3, 64, 64], replicated, may hold values from -0.15625 to 0.15625
- w_down: bfloat16 [2, 2, 2, 64, 128], replicated, may hold values from -0.25 to 0.25
- w_point: bfloat16 [128, 256], replicated, may hold values from -0.5 to 0.5
- cotangent: bfloat16 [4, 512, 64, 256], P('dp', 'brick'), may hold values from -0.015625 to 0.015625
Outputs:
- grad_w_conv: float32 [3, 3, 3, 64, 64], replicated
- grad_w_down: float32 [2, 2, 2, 64, 128], replicated
- grad_w_point: float32 [128, 256], replicated
Inputs may be any that keep to these rules, and one draw needn't show every extreme that they name: `neighbours`: bricks of a scene form a lattice of 128 x 4 x 1 bricks, 8 consecutive ids a device; an entry names the lattice neighbour at its column's offset or is -1; column 13 is the brick itself. Columns with first offset 0 name bricks of the same device, offset -1 of the same or the previous device, offset +1 of the same or the next. `owners`: within a scene a permutation of the coarse slots; a slot's device is slot // 8. A device hands exactly 1 bricks to each device it hands any to.
All inputs are finite; a program needn't handle non-finite values. No bound on the sum of `occupancy` on one device may be relied on, other than what follows from the above.
Results may differ from a plain program's by a relative error of at most 0.012.
Values may be sent and summed in bfloat16 or wider, within the bound.
A program may use at most 64 MiB of HBM per device.

v0:
```python
import jax
import jax.numpy as jnp
from jax import lax
from jax.sharding import PartitionSpec as P

SPANS = ((7, 8), (0, 8), (0, 1))


def extended(shard, sides, width):
    for axis, dim in sides:
        peers, length = (lax.axis_size(axis), shard.shape[dim])
        up = [(i, (i + 1) % peers) for i in range(peers - 1)]
        down = [(j, i) for i, j in up]
        last = lax.slice_in_dim(shard, length - width, length, axis=dim)
        initial = lax.slice_in_dim(shard, 0, width, axis=dim)
        before = lax.ppermute(last, axis, up)
        after = lax.ppermute(initial, axis, down)
        shard = jnp.concatenate([before, shard, after], axis=dim)
    return shard


def assemble(pools, indices):
    planes = []
    for a in range(3):
        row_parts = []
        for b in range(3):
            col_parts = []
            for c in range(3):
                window_part = pools[a][
                    :, :, SPANS[b][0] : SPANS[b][1], SPANS[c][0] : SPANS[c][1], :
                ]
                col_parts.append(
                    jnp.take(window_part, indices[a][:, 9 * a + 3 * b + c], axis=0, mode="clip")
                )
            row_parts.append(jnp.concatenate(col_parts, axis=3))
        planes.append(jnp.concatenate(row_parts, axis=2))
    return jnp.concatenate(planes, axis=1)


def silu_slope(signal):
    gate_value = jax.nn.sigmoid(signal)
    return gate_value * (1.0 + signal * (1.0 - gate_value))


def point_layer(rows_in, cot_rows, w_point):
    brick_count = rows_in.shape[0]
    row_block = rows_in.reshape(-1, w_point.shape[0])
    point_act = jnp.dot(row_block, w_point, preferred_element_type=jnp.float32)
    grad_point = (
        cot_rows.reshape(point_act.shape).astype(jnp.float32) * silu_slope(point_act)
    ).astype(jnp.bfloat16)
    grad_weight = lax.dot_general(
        row_block, grad_point, (((0,), (0,)), ((), ())), preferred_element_type=jnp.float32
    )
    grad_rows = lax.dot_general(
        grad_point, w_point, (((1,), (1,)), ((), ())), preferred_element_type=jnp.float32
    )
    return (grad_rows.astype(jnp.bfloat16).reshape(brick_count, -1), grad_weight)


def shards(features, occupancy, neighbours, owners, w_conv, w_down, w_point, cotangent):
    brick_count = features.shape[1]
    in_width = features.shape[3]
    brick_devices = lax.axis_size("brick")
    device_pos = lax.axis_index("brick")
    bricks = features[0].reshape(brick_count, 8, 8, 8, in_width)
    link_table = neighbours[0]
    linked = link_table >= 0
    local_ids = link_table - device_pos * brick_count
    zero_brick = jnp.zeros((1, 8, 8, 8, in_width), bricks.dtype)
    beside_all = extended(bricks, (("brick", 0),), brick_count)
    brick_pool = jnp.concatenate([beside_all, zero_brick], axis=0)
    pool_index = jnp.where(linked, local_ids + brick_count, 3 * brick_count)
    padded = assemble(
        (brick_pool[:, 7:8], brick_pool, brick_pool[:, 0:1]), (pool_index, pool_index, pool_index)
    )
    pre_act = lax.conv_general_dilated(
        padded,
        w_conv,
        (1, 1, 1),
        "VALID",
        dimension_numbers=("NDHWC", "DHWIO", "NDHWC"),
        preferred_element_type=jnp.float32,
    )
    occupied = occupancy[0].reshape(brick_count, 8, 8, 8, 1).astype(jnp.float32)
    hidden = (jax.nn.silu(pre_act) * occupied).astype(jnp.bfloat16)
    grouped = hidden.reshape(brick_count, 4, 2, 4, 2, 4, 2, in_width)
    down_act = jnp.einsum(
        "bpiqjrkc,ijkcd->bpqrd", grouped, w_down, preferred_element_type=jnp.float32
    )
    coarse = jax.nn.silu(down_act).astype(jnp.bfloat16).reshape(brick_count, -1)
    target_dev = owners[0] // brick_count
    recv_slot = owners[0] % brick_count
    capacity = max(1, brick_count // brick_devices)
    dest_hits = (target_dev[:, None] == jnp.arange(brick_devices, dtype=jnp.int32)[None, :]).astype(
        jnp.int32
    )
    earlier_hits = jnp.cumsum(dest_hits, axis=0) - dest_hits
    rank_in = jnp.sum(earlier_hits * dest_hits, axis=1)
    position = target_dev * capacity + rank_in
    slot_out = jnp.full((brick_devices * capacity,), -1, jnp.int32).at[position].set(recv_slot)
    arrived = lax.all_to_all(slot_out, "brick", split_axis=0, concat_axis=0, tiled=True)
    present = arrived >= 0
    safe_slots = jnp.where(present, arrived, 0)
    send_rows = (
        jnp.zeros((brick_devices * capacity, coarse.shape[1]), jnp.bfloat16)
        .at[position]
        .set(coarse)
    )
    landed = lax.all_to_all(send_rows, "brick", split_axis=0, concat_axis=0, tiled=True)
    drop_slots = jnp.where(present, arrived, brick_count)
    placed = jnp.zeros_like(coarse).at[drop_slots].set(landed, mode="drop")
    grad_placed, grad_w_point = point_layer(placed, cotangent[0], w_point)
    reply = jnp.where(
        present[:, None], jnp.take(grad_placed, safe_slots, axis=0), jnp.zeros((), jnp.bfloat16)
    )
    returned = lax.all_to_all(reply, "brick", split_axis=0, concat_axis=0, tiled=True)
    grad_coarse = jnp.take(returned, position, axis=0)
    grad_down = (
        grad_coarse.reshape(down_act.shape).astype(jnp.float32) * silu_slope(down_act)
    ).astype(jnp.bfloat16)
    grad_w_down = jnp.einsum(
        "bpiqjrkc,bpqrd->ijkcd", grouped, grad_down, preferred_element_type=jnp.float32
    )
    grad_hidden = jnp.einsum(
        "bpqrd,ijkcd->bpiqjrkc", grad_down, w_down, preferred_element_type=jnp.float32
    )
    grad_hidden = grad_hidden.reshape(brick_count, 8, 8, 8, in_width)
    grad_pre = (grad_hidden * occupied * silu_slope(pre_act)).astype(jnp.bfloat16)
    flat_grad = grad_pre.reshape(-1, in_width)
    term_list = []
    for a in range(3):
        for b in range(3):
            for c in range(3):
                window_part = padded[:, a : a + 8, b : b + 8, c : c + 8, :].reshape(-1, in_width)
                term_list.append(
                    lax.dot_general(
                        window_part,
                        flat_grad,
                        (((0,), (0,)), ((), ())),
                        preferred_element_type=jnp.float32,
                    )
                )
    grad_w_conv = jnp.stack(term_list).reshape(3, 3, 3, in_width, in_width)
    summed = lax.psum((grad_w_conv, grad_w_down, grad_w_point), ("dp", "brick"))
    return (summed[0], summed[1], summed[2])


def solution(mesh):
    in_specs = (
        P("dp", "brick", None, None),
        P("dp", "brick", None),
        P("dp", "brick", None),
        P("dp", "brick"),
        P(),
        P(),
        P(),
        P("dp", "brick", None, None),
    )
    out_specs = (P(), P(), P())
    return jax.shard_map(shards, mesh=mesh, in_specs=in_specs, out_specs=out_specs, check_vma=False)
```

profile of v0, /device:TPU:97, one launch (start us, length us, event | category | flops | bytes accessed | tf_op | source)
XLA Modules:
  0.0 517.1 jit_solution(3569445359638503586)
XLA Ops:
  7.2 1.9 copy.274
  9.1 3.7 collective-permute-start
  12.7 1.9 collective-permute-start.1
  17.6 11.8 %all-to-all-start = ((s32[64,1,1]{2,1,0:T(1,128)}), s32[64,1,1]{2,1,0:T(1,128)S(1)}, u32[]{:S(2)}, u32[]{:S(2)}) async-start(s32[64,1,1]{2,1,0:T(1,128)} %copy.303), calls=%async_computation | async-start | bytes 65536 | tf_op jit(solution)/shard_map/all_to_all | solution.py:102
  42.8 2.9 maximum_maximum_fusion
  48.7 3.0 copy.293
  52.6 1.6 gather_fusion.14
  55.2 1.6 gather_fusion.12
  75.9 2.8 gather_fusion.13
  80.6 2.1 gather_fusion.7
  82.7 1.3 copy.422
  84.0 1.5 copy.281
  85.5 2.1 gather_fusion.5
  87.6 1.3 copy.423
  88.9 1.5 copy.277
  90.4 2.1 gather_fusion.3
  92.4 1.3 copy.424
  94.4 1.5 gather_fusion.1
  96.8 1.7 gather_fusion.4
  98.6 1.4 gather_fusion.8
  100.1 1.4 gather_fusion.18
  101.5 1.4 gather_fusion.20
  102.8 1.4 gather_fusion.24
  104.2 1.4 gather_fusion.26
  105.6 1.4 gather_fusion.6
  107.0 1.4 gather_fusion.2
  108.4 1.4 gather_fusion
  109.8 6.8 %multiply_convert_fusion.1 = (bf16[8,8,8,8,64]{4,0,3,2,1:T(8,128)(2,1)S(1)}, f32[8,8,8,8,64]{4,0,3,2,1:T(8,128)}) fusion(f32[8,8,8,8]{0,3,2,1:T(8,128)} %bitcast.539, bf16[3,3,3,64,64]{4,3,2,1,0:T(8,128)(2,1)S(1)} %copy-done, bf16[8,1,1,1,64]{4,0,3,2,1:T(8,128)(2,1)S(1)} %bitcast.601, bf16[8,1,1,8,64]{4,0,3,2,1:T(8,128)(2,1)} %bitcast.573, ...), kind=kOutput, calls=%fused_computation.34 | convolution fusion | flops 920854528 | bytes 2834432 | tf_op jit(solution)/shard_map/conv_general_dilated | solution.py:77
  117.8 1.5 scatter_custom_fusion.1
  119.8 2.1 reduce.56
  121.9 2.6 reshape.781
  124.5 10.3 %all-to-all-start.1 = ((bf16[64,2,4096]{2,1,0:T(2,128)(2,1)}), bf16[64,2,4096]{2,1,0:T(2,128)(2,1)S(1)}, u32[]{:S(2)}, u32[]{:S(2)}) async-start(bf16[64,2,4096]{2,1,0:T(2,128)(2,1)} %reshape.781), calls=%async_computation.1 | async-start | bytes 2097152 | tf_op jit(solution)/shard_map/all_to_all | solution.py:110
  134.9 26.5 %all-to-all-done.1 = bf16[64,2,4096]{2,1,0:T(2,128)(2,1)S(1)} async-done(((bf16[64,2,4096]{2,1,0:T(2,128)(2,1)}), bf16[64,2,4096]{2,1,0:T(2,128)(2,1)S(1)}, u32[]{:S(2)}, u32[]{:S(2)}) %all-to-all-start.1) | async-done | bytes 1048608 | tf_op jit(solution)/shard_map/all_to_all | solution.py:110
  161.4 3.5 reshape.782
  164.9 4.0 scatter_custom_fusion.2
  171.3 1.3 gather_fusion.27
  173.8 2.7 reduce.57
  176.5 1.6 reshape.783
  178.1 7.9 %all-to-all-start.2 = ((bf16[64,2,4096]{2,1,0:T(2,128)(2,1)}), bf16[64,2,4096]{2,1,0:T(2,128)(2,1)S(1)}, u32[]{:S(2)}, u32[]{:S(2)}) async-start(bf16[64,2,4096]{2,1,0:T(2,128)(2,1)} %reshape.783), calls=%async_computation.2 | async-start | bytes 2097152 | tf_op jit(solution)/shard_map/all_to_all | solution.py:117
  190.5 6.2 %maximum_maximum_fusion.2 = bf16[8,9,10,10,64]{4,0,3,2,1:T(8,128)(2,1)} fusion(bf16[8,1,1,1,64]{4,0,3,2,1:T(8,128)(2,1)} %bitcast.602, bf16[8,1,1,8,64]{4,0,3,2,1:T(8,128)(2,1)S(1)} %bitcast.574, bf16[8,1,1,1,64]{4,0,3,2,1:T(8,128)(2,1)} %bitcast.598, bf16[8,1,8,1,64]{4,0,3,2,1:T(8,128)(2,1)S(1)} %bitcast.576, bf16[8,1,8,8,64]{4,0,3,2,1:T(8,128)(2,1)S(1)} %bitcast.545, ...), kind=kLoop, calls=%fused_computation.91 | loop fusion | flops 7833600 | bytes 1843200 | tf_op jit(solution)/shard_map/concatenate | solution.py:37
  196.7 3.3 maximum_maximum_fusion.1
  200.9 11.7 %all-to-all-done.2 = bf16[64,2,4096]{2,1,0:T(2,128)(2,1)S(1)} async-done(((bf16[64,2,4096]{2,1,0:T(2,128)(2,1)}), bf16[64,2,4096]{2,1,0:T(2,128)(2,1)S(1)}, u32[]{:S(2)}, u32[]{:S(2)}) %all-to-all-start.2) | async-done | bytes 1048608 | tf_op jit(solution)/shard_map/all_to_all | solution.py:117
  212.6 3.5 reshape.784
  216.1 2.8 copy.406
  219.6 1.8 convolution_bitcast_fusion.1
  243.7 261.8 %all-reduce.3.cloned.1.call-done = (f32[3,3,3,64,64]{4,3,2,1,0:T(8,128)}, f32[2,2,2,64,128]{4,3,0,1,2:T(8,128)}, f32[128,256]{1,0:T(8,128)}) async-done(((f32[3,3,3,64,64]{4,3,2,1,0:T(8,128)}, f32[2,2,2,64,128]{4,3,0,1,2:T(8,128)}, f32[128,256]{1,0:T(8,128)}), (f32[3,3,3,64,64]{4,3,2,1,0:T(8,128)}, f32[2,2,2,64,128]{4,3,0,1,2:T(8,128)}, f32[128,256]{1,0:T(8,128)})) %all-reduce.3.cloned.1.call-update) | async-done | bytes 835600 | tf_op jit(solution)/shard_map/psum | solution.py:145
  505.5 1.7 copy.325
  507.2 2.2 copy.457
  (240 shorter events, 77.7 us)
Async XLA Ops:
  7.2 102.6 %copy-start = (bf16[3,3,3,64,64]{4,3,2,1,0:T(8,128)(2,1)S(1)}, bf16[3,3,3,64,64]{4,3,2,1,0:T(8,128)(2,1)}, u32[]{:S(2)}) copy-start(bf16[3,3,3,64,64]{4,3,2,1,0:T(8,128)(2,1)} %param.12) | copy-start | bytes 663556
  9.1 33.8 %collective-permute-start = (bf16[8,8,8,8,64]{4,0,3,2,1:T(8,128)(2,1)S(1)}, bf16[8,8,8,8,64]{4,0,3,2,1:T(8,128)(2,1)S(1)}, u32[]{:S(2)}, u32[]{:S(2)}) collective-permute-start(bf16[8,8,8,8,64]{4,0,3,2,1:T(8,128)(2,1)S(1)} %bitcast.503), channel_id=1, source_target_pairs={{0,1},{1,2},{2,3},{3,4},{4,5},{5,6},{6,7},{7,8},{8,9},{9,10},{10,1... | collective-permute-start | bytes 1572872 | tf_op jit(solution)/shard_map/ppermute | solution.py:16
  12.7 30.1 %collective-permute-start.1 = (bf16[8,8,8,8,64]{4,0,3,2,1:T(8,128)(2,1)S(1)}, bf16[8,8,8,8,64]{4,0,3,2,1:T(8,128)(2,1)}, u32[]{:S(2)}, u32[]{:S(2)}) collective-permute-start(bf16[8,8,8,8,64]{4,0,3,2,1:T(8,128)(2,1)S(1)} %bitcast.504), channel_id=1, source_target_pairs={{1,0},{2,1},{3,2},{4,3},{5,4},{6,5},{7,6},{8,7},{9,8},{10,9},{11,1... | collective-permute-start | bytes 1572872 | tf_op jit(solution)/shard_map/ppermute | solution.py:17
  15.3 2.3 copy-start.47
  15.6 2.0 copy-start.50
  17.6 22.8 %all-to-all-start = ((s32[64,1,1]{2,1,0:T(1,128)}), s32[64,1,1]{2,1,0:T(1,128)S(1)}, u32[]{:S(2)}, u32[]{:S(2)}) async-start(s32[64,1,1]{2,1,0:T(1,128)} %copy.303), calls=%async_computation | async-start | bytes 65536 | tf_op jit(solution)/shard_map/all_to_all | solution.py:102
  41.6 4.1 copy-start.48
  58.3 14.6 %copy-start.21 = (bf16[25,8,64]{2,0,1:T(8,128)(2,1)S(1)}, bf16[25,8,64]{2,0,1:T(8,128)(2,1)}, u32[]{:S(2)}) copy-start(bf16[25,8,64]{2,0,1:T(8,128)(2,1)} %get-tuple-element.47) | copy-start | bytes 76804
  64.9 44.9 %copy-start.6 = (bf16[8,8,8,64]{3,0,2,1:T(8,128)(2,1)}, bf16[8,8,8,64]{3,0,2,1:T(8,128)(2,1)S(1)}, u32[]{:S(2)}) copy-start(bf16[8,8,8,64]{3,0,2,1:T(8,128)(2,1)S(1)} %copy.409) | copy-start | bytes 196612
  78.7 20.0 %copy-start.1 = (bf16[8,8,8,8,64]{4,3,2,1,0:T(8,128)(2,1)}, bf16[8,8,8,8,64]{4,3,2,1,0:T(8,128)(2,1)S(1)}, u32[]{:S(2)}) copy-start(bf16[8,8,8,8,64]{4,3,2,1,0:T(8,128)(2,1)S(1)} %gather_fusion.13) | copy-start | bytes 1572868
  95.9 20.7 %copy-start.32 = (bf16[8,8,64]{2,0,1:T(8,128)(2,1)}, bf16[8,8,64]{2,0,1:T(8,128)(2,1)S(1)}, u32[]{:S(2)}) copy-start(bf16[8,8,64]{2,0,1:T(8,128)(2,1)S(1)} %copy.425) | copy-start | bytes 24580
  98.6 18.0 %copy-start.14 = (bf16[8,8,8,64]{3,0,2,1:T(8,128)(2,1)}, bf16[8,8,8,64]{3,0,2,1:T(8,128)(2,1)S(1)}, u32[]{:S(2)}) copy-start(bf16[8,8,8,64]{3,0,2,1:T(8,128)(2,1)S(1)} %copy.413) | copy-start | bytes 196612
  100.1 16.6 %copy-start.35 = (bf16[8,64]{1,0:T(8,128)(2,1)}, bf16[8,64]{1,0:T(8,128)(2,1)S(1)}, u32[]{:S(2)}) copy-start(bf16[8,64]{1,0:T(8,128)(2,1)S(1)} %gather_fusion.8) | copy-start | bytes 3076
  101.4 15.2 %copy-start.37 = (bf16[8,64]{1,0:T(8,128)(2,1)}, bf16[8,64]{1,0:T(8,128)(2,1)S(1)}, u32[]{:S(2)}) copy-start(bf16[8,64]{1,0:T(8,128)(2,1)S(1)} %gather_fusion.18) | copy-start | bytes 3076
  102.8 13.8 %copy-start.38 = (bf16[8,64]{1,0:T(8,128)(2,1)}, bf16[8,64]{1,0:T(8,128)(2,1)S(1)}, u32[]{:S(2)}) copy-start(bf16[8,64]{1,0:T(8,128)(2,1)S(1)} %gather_fusion.20) | copy-start | bytes 3076
  104.2 12.4 %copy-start.41 = (bf16[8,64]{1,0:T(8,128)(2,1)}, bf16[8,64]{1,0:T(8,128)(2,1)S(1)}, u32[]{:S(2)}) copy-start(bf16[8,64]{1,0:T(8,128)(2,1)S(1)} %gather_fusion.24) | copy-start | bytes 3076
  105.6 11.0 %copy-start.44 = (bf16[8,64]{1,0:T(8,128)(2,1)}, bf16[8,64]{1,0:T(8,128)(2,1)S(1)}, u32[]{:S(2)}) copy-start(bf16[8,64]{1,0:T(8,128)(2,1)S(1)} %gather_fusion.26) | copy-start | bytes 3076
  107.0 9.6 %copy-start.39 = (bf16[8,64]{1,0:T(8,128)(2,1)}, bf16[8,64]{1,0:T(8,128)(2,1)S(1)}, u32[]{:S(2)}) copy-start(bf16[8,64]{1,0:T(8,128)(2,1)S(1)} %gather_fusion.6) | copy-start | bytes 3076
  108.4 8.3 %copy-start.42 = (bf16[8,64]{1,0:T(8,128)(2,1)}, bf16[8,64]{1,0:T(8,128)(2,1)S(1)}, u32[]{:S(2)}) copy-start(bf16[8,64]{1,0:T(8,128)(2,1)S(1)} %gather_fusion.2) | copy-start | bytes 3076
  109.8 6.9 %copy-start.45 = (bf16[8,64]{1,0:T(8,128)(2,1)}, bf16[8,64]{1,0:T(8,128)(2,1)S(1)}, u32[]{:S(2)}) copy-start(bf16[8,64]{1,0:T(8,128)(2,1)S(1)} %gather_fusion) | copy-start | bytes 3076
  109.8 6.9 %copy-start.24 = (bf16[2,2,2,64,128]{4,3,2,1,0:T(8,128)(2,1)S(1)}, bf16[2,2,2,64,128]{4,3,2,1,0:T(8,128)(2,1)}, u32[]{:S(2)}) copy-start(bf16[2,2,2,64,128]{4,3,2,1,0:T(8,128)(2,1)} %param.13) | copy-start | bytes 393220
  121.9 12.9 %copy-start.49 = (s32[64]{0:T(128)S(1)}, s32[64]{0:T(128)}, u32[]{:S(2)}) copy-start(s32[64]{0:T(128)} %copy-done.48) | copy-start | bytes 772
  124.5 36.9 %all-to-all-start.1 = ((bf16[64,2,4096]{2,1,0:T(2,128)(2,1)}), bf16[64,2,4096]{2,1,0:T(2,128)(2,1)S(1)}, u32[]{:S(2)}, u32[]{:S(2)}) async-start(bf16[64,2,4096]{2,1,0:T(2,128)(2,1)} %reshape.781), calls=%async_computation.1 | async-start | bytes 2097152 | tf_op jit(solution)/shard_map/all_to_all | solution.py:110
  134.9 34.8 %copy-start.34 = (bf16[128,256]{1,0:T(8,128)(2,1)S(1)}, bf16[128,256]{1,0:T(8,128)(2,1)}, u32[]{:S(2)}) copy-start(bf16[128,256]{1,0:T(8,128)(2,1)} %param.14) | copy-start | bytes 196612
  176.4 14.0 %copy-start.7 = (bf16[8,8,8,64]{3,0,2,1:T(8,128)(2,1)S(1)}, bf16[8,8,8,64]{3,0,2,1:T(8,128)(2,1)}, u32[]{:S(2)}) copy-start(bf16[8,8,8,64]{3,0,2,1:T(8,128)(2,1)} %copy-done.6) | copy-start | bytes 196612
  176.5 14.0 %copy-start.8 = (bf16[8,8,8,64]{3,0,2,1:T(8,128)(2,1)S(1)}, bf16[8,8,8,64]{3,0,2,1:T(8,128)(2,1)}, u32[]{:S(2)}) copy-start(bf16[8,8,8,64]{3,0,2,1:T(8,128)(2,1)} %copy.412) | copy-start | bytes 196612
  176.5 14.0 %copy-start.13 = (bf16[8,8,8,64]{3,0,2,1:T(8,128)(2,1)S(1)}, bf16[8,8,8,64]{3,0,2,1:T(8,128)(2,1)}, u32[]{:S(2)}) copy-start(bf16[8,8,8,64]{3,0,2,1:T(8,128)(2,1)} %copy.408) | copy-start | bytes 196612
  176.5 13.9 %copy-start.22 = (bf16[8,8,64]{2,0,1:T(8,128)(2,1)S(1)}, bf16[8,8,64]{2,0,1:T(8,128)(2,1)}, u32[]{:S(2)}) copy-start(bf16[8,8,64]{2,0,1:T(8,128)(2,1)} %copy.420) | copy-start | bytes 24580
  176.5 13.9 %copy-start.23 = (bf16[8,8,64]{2,0,1:T(8,128)(2,1)S(1)}, bf16[8,8,64]{2,0,1:T(8,128)(2,1)}, u32[]{:S(2)}) copy-start(bf16[8,8,64]{2,0,1:T(8,128)(2,1)} %copy.421) | copy-start | bytes 24580
  176.5 13.9 %copy-start.27 = (bf16[8,8,64]{2,0,1:T(8,128)(2,1)S(1)}, bf16[8,8,64]{2,0,1:T(8,128)(2,1)}, u32[]{:S(2)}) copy-start(bf16[8,8,64]{2,0,1:T(8,128)(2,1)} %copy.414) | copy-start | bytes 24580
  176.5 13.9 %copy-start.28 = (bf16[8,8,64]{2,0,1:T(8,128)(2,1)S(1)}, bf16[8,8,64]{2,0,1:T(8,128)(2,1)}, u32[]{:S(2)}) copy-start(bf16[8,8,64]{2,0,1:T(8,128)(2,1)} %copy.415) | copy-start | bytes 24580
  178.1 34.5 %all-to-all-start.2 = ((bf16[64,2,4096]{2,1,0:T(2,128)(2,1)}), bf16[64,2,4096]{2,1,0:T(2,128)(2,1)S(1)}, u32[]{:S(2)}, u32[]{:S(2)}) async-start(bf16[64,2,4096]{2,1,0:T(2,128)(2,1)} %reshape.783), calls=%async_computation.2 | async-start | bytes 2097152 | tf_op jit(solution)/shard_map/all_to_all | solution.py:117
  186.0 319.5 %all-reduce.3.cloned.1.call-start = ((), (), s32[]{:S(2)}) async-start(), calls=%async_computation.3 | async-start | bytes 2555904 | tf_op jit(solution)/shard_map/psum | solution.py:145
  189.4 7.2 %copy-start.15 = (bf16[8,8,8,64]{3,0,2,1:T(8,128)(2,1)S(1)}, bf16[8,8,8,64]{3,0,2,1:T(8,128)(2,1)}, u32[]{:S(2)}) copy-start(bf16[8,8,8,64]{3,0,2,1:T(8,128)(2,1)} %copy-done.14) | copy-start | bytes 196612
  189.4 7.2 %copy-start.29 = (bf16[8,8,64]{2,0,1:T(8,128)(2,1)S(1)}, bf16[8,8,64]{2,0,1:T(8,128)(2,1)}, u32[]{:S(2)}) copy-start(bf16[8,8,64]{2,0,1:T(8,128)(2,1)} %copy.422) | copy-start | bytes 24580
  189.4 7.2 %copy-start.30 = (bf16[8,8,64]{2,0,1:T(8,128)(2,1)S(1)}, bf16[8,8,64]{2,0,1:T(8,128)(2,1)}, u32[]{:S(2)}) copy-start(bf16[8,8,64]{2,0,1:T(8,128)(2,1)} %copy.423) | copy-start | bytes 24580
  189.4 7.2 %copy-start.31 = (bf16[8,8,64]{2,0,1:T(8,128)(2,1)S(1)}, bf16[8,8,64]{2,0,1:T(8,128)(2,1)}, u32[]{:S(2)}) copy-start(bf16[8,8,64]{2,0,1:T(8,128)(2,1)} %copy.424) | copy-start | bytes 24580
  189.5 7.2 %copy-start.33 = (bf16[8,8,64]{2,0,1:T(8,128)(2,1)S(1)}, bf16[8,8,64]{2,0,1:T(8,128)(2,1)}, u32[]{:S(2)}) copy-start(bf16[8,8,64]{2,0,1:T(8,128)(2,1)} %copy-done.32) | copy-start | bytes 24580
  189.5 7.2 %copy-start.36 = (bf16[8,64]{1,0:T(8,128)(2,1)S(1)}, bf16[8,64]{1,0:T(8,128)(2,1)}, u32[]{:S(2)}) copy-start(bf16[8,64]{1,0:T(8,128)(2,1)} %copy-done.35) | copy-start | bytes 3076
  189.5 7.2 %copy-start.40 = (bf16[8,64]{1,0:T(8,128)(2,1)S(1)}, bf16[8,64]{1,0:T(8,128)(2,1)}, u32[]{:S(2)}) copy-start(bf16[8,64]{1,0:T(8,128)(2,1)} %copy-done.39) | copy-start | bytes 3076
  189.5 7.2 %copy-start.43 = (bf16[8,64]{1,0:T(8,128)(2,1)S(1)}, bf16[8,64]{1,0:T(8,128)(2,1)}, u32[]{:S(2)}) copy-start(bf16[8,64]{1,0:T(8,128)(2,1)} %copy-done.42) | copy-start | bytes 3076
  189.5 7.2 %copy-start.46 = (bf16[8,64]{1,0:T(8,128)(2,1)S(1)}, bf16[8,64]{1,0:T(8,128)(2,1)}, u32[]{:S(2)}) copy-start(bf16[8,64]{1,0:T(8,128)(2,1)} %copy-done.45) | copy-start | bytes 3076
  196.7 3.3 copy-start.17
  216.1 3.5 copy-start.10
  216.1 3.5 copy-start.52
  219.6 1.8 copy-start.25
  222.6 1.6 copy-start.11
  505.5 3.9 copy-start.26
  (12 other events, 13.9 us)
Sparse Core Ops, SparseCore 0:
  243.8 261.6 all-reduce.2
where the time goes:
time: 523 us; the launch traced here: 517 us
  waiting for transfers between devices  300 us (57%)
  local copies, waits for them, and re-layouts  104 us (20%)
  starting transfers between devices  35.6 us (7%)
  other arithmetic  35.2 us (7%)
  matrix products  26.6 us (5%)
  between operations  15.2 us (3%)
    psum x1, waiting for transfers between devices, shards(): summed = lax.psum((grad_w_conv, grad_w_down, grad_w_point), ('dp', 'brick'))  262 us
    gather x48, local copies, waits for them, and re-layouts, assemble(): jnp.take(window_part, indices[a][:, 9 * a + 3 * b + c], axis=0, mode='clip')  46 us
    all_to_all x1, waiting for transfers between devices, shards(): lax.all_to_all(send_rows, 'brick', split_axis=0, concat_axis=0, tiled=True)  26.5 us
    unnamed x117, local copies, waits for them, and re-layouts  26.5 us
    slice x22, local copies, waits for them, and re-layouts, assemble(): pools[a][:, :, SPANS[b][0]:SPANS[b][1], SPANS[c][0]:SPANS[c][1], :]  15.4 us
    dot_general x27, matrix products, shards(): lax.dot_general(window_part, flat_grad, (((0,), (0,)), ((), ())), preferr...  14.9 us
    all_to_all x1, starting transfers between devices, shards(): lax.all_to_all(slot_out, 'brick', split_axis=0, concat_axis=0, tiled=True)  11.8 us
    all_to_all x1, waiting for transfers between devices, shards(): lax.all_to_all(reply, 'brick', split_axis=0, concat_axis=0, tiled=True)  11.7 us
  transfers between devices with their start and end apart: 6, of which 3 were waited for; matrix products, arithmetic and copies ran while one was open for 6% of the time, Pallas kernels for 0%

commit v1 on v0

--- a/solution.py
+++ b/solution.py
@@ -142,7 +142,7 @@
                     )
                 )
     grad_w_conv = jnp.stack(term_list).reshape(3, 3, 3, in_width, in_width)
-    summed = lax.psum((grad_w_conv, grad_w_down, grad_w_point), ("dp", "brick"))
+    summed = lax.psum(lax.psum((grad_w_conv, grad_w_down, grad_w_point), "dp"), "brick")
     return (summed[0], summed[1], summed[2])
 
 

time: 523 us -> 507 us (0.969)
  waiting for transfers between devices: 300 us -> 284 us
    psum x1 -> x2, waiting for transfers between devices: 262 us -> 246 us  [the longest x1 195 us: shards(): lax.psum(lax.psum((grad_w_conv, grad_w_down, grad_w_point), 'dp'), 'brick')]
  transfers between devices with their start and end apart: 6 -> 7, of which waited for: 3 -> 4; matrix products, arithmetic and copies ran while one was open for 6% -> 6% of each run, Pallas kernels for 0% -> 0%
where the time goes in v1:
time: 507 us; the launch traced here: 501 us
  waiting for transfers between devices  284 us (56%)
  local copies, waits for them, and re-layouts  104 us (21%)
  starting transfers between devices  35.7 us (7%)
  other arithmetic  35.2 us (7%)
  matrix products  26.6 us (5%)
  between operations  15.3 us (3%)
    psum x1, waiting for transfers between devices, shards(): lax.psum(lax.psum((grad_w_conv, grad_w_down, grad_w_point), 'dp'), 'brick')  195 us
    psum x1, waiting for transfers between devices, shards(): lax.psum((grad_w_conv, grad_w_down, grad_w_point), 'dp')  50.9 us
    gather x48, local copies, waits for them, and re-layouts, assemble(): jnp.take(window_part, indices[a][:, 9 * a + 3 * b + c], axis=0, mode='clip')  46 us
    all_to_all x1, waiting for transfers between devices, shards(): lax.all_to_all(send_rows, 'brick', split_axis=0, concat_axis=0, tiled=True)  26.5 us
    unnamed x117, local copies, waits for them, and re-layouts  26.5 us
    slice x22, local copies, waits for them, and re-layouts, assemble(): pools[a][:, :, SPANS[b][0]:SPANS[b][1], SPANS[c][0]:SPANS[c][1], :]  15.4 us
    dot_general x27, matrix products, shards(): lax.dot_general(window_part, flat_grad, (((0,), (0,)), ((), ())), preferr...  14.9 us
    all_to_all x1, starting transfers between devices, shards(): lax.all_to_all(slot_out, 'brick', split_axis=0, concat_axis=0, tiled=True)  11.8 us
  transfers between devices with their start and end apart: 7, of which 4 were waited for; matrix products, arithmetic and copies ran while one was open for 6% of the time, Pallas kernels for 0%

profile of v1, /device:TPU:97, one launch (start us, length us, event | category | flops | bytes accessed | tf_op | source)
XLA Modules:
  0.0 501.0 jit_solution(14554308801052425694)
XLA Ops:
  7.2 1.9 copy.274
  9.1 3.7 collective-permute-start
  12.7 1.9 collective-permute-start.1
  17.6 11.8 %all-to-all-start = ((s32[64,1,1]{2,1,0:T(1,128)}), s32[64,1,1]{2,1,0:T(1,128)S(1)}, u32[]{:S(2)}, u32[]{:S(2)}) async-start(s32[64,1,1]{2,1,0:T(1,128)} %copy.303), calls=%async_computation | async-start | bytes 65536 | tf_op jit(solution)/shard_map/all_to_all | solution.py:102
  42.8 2.9 maximum_maximum_fusion
  48.7 3.0 copy.293
  52.6 1.6 gather_fusion.14
  55.2 1.6 gather_fusion.12
  75.9 2.8 gather_fusion.13
  80.6 2.1 gather_fusion.7
  82.7 1.3 copy.422
  84.0 1.5 copy.281
  85.5 2.1 gather_fusion.5
  87.6 1.3 copy.423
  88.9 1.5 copy.277
  90.4 2.1 gather_fusion.3
  94.4 1.5 gather_fusion.1
  96.8 1.7 gather_fusion.4
  98.6 1.4 gather_fusion.8
  100.1 1.4 gather_fusion.18
  101.5 1.4 gather_fusion.20
  102.8 1.4 gather_fusion.24
  104.2 1.4 gather_fusion.26
  105.6 1.4 gather_fusion.6
  107.0 1.4 gather_fusion.2
  108.4 1.4 gather_fusion
  109.8 6.8 %multiply_convert_fusion.1 = (bf16[8,8,8,8,64]{4,0,3,2,1:T(8,128)(2,1)S(1)}, f32[8,8,8,8,64]{4,0,3,2,1:T(8,128)}) fusion(f32[8,8,8,8]{0,3,2,1:T(8,128)} %bitcast.539, bf16[3,3,3,64,64]{4,3,2,1,0:T(8,128)(2,1)S(1)} %copy-done, bf16[8,1,1,1,64]{4,0,3,2,1:T(8,128)(2,1)S(1)} %bitcast.601, bf16[8,1,1,8,64]{4,0,3,2,1:T(8,128)(2,1)} %bitcast.573, ...), kind=kOutput, calls=%fused_computation.34 | convolution fusion | flops 920854528 | bytes 2834432 | tf_op jit(solution)/shard_map/conv_general_dilated | solution.py:77
  117.8 1.5 scatter_custom_fusion.1
  119.8 2.1 reduce.56
  121.9 2.6 reshape.781
  124.5 10.3 %all-to-all-start.1 = ((bf16[64,2,4096]{2,1,0:T(2,128)(2,1)}), bf16[64,2,4096]{2,1,0:T(2,128)(2,1)S(1)}, u32[]{:S(2)}, u32[]{:S(2)}) async-start(bf16[64,2,4096]{2,1,0:T(2,128)(2,1)} %reshape.781), calls=%async_computation.1 | async-start | bytes 2097152 | tf_op jit(solution)/shard_map/all_to_all | solution.py:110
  134.9 26.5 %all-to-all-done.1 = bf16[64,2,4096]{2,1,0:T(2,128)(2,1)S(1)} async-done(((bf16[64,2,4096]{2,1,0:T(2,128)(2,1)}), bf16[64,2,4096]{2,1,0:T(2,128)(2,1)S(1)}, u32[]{:S(2)}, u32[]{:S(2)}) %all-to-all-start.1) | async-done | bytes 1048608 | tf_op jit(solution)/shard_map/all_to_all | solution.py:110
  161.4 3.5 reshape.782
  164.9 4.0 scatter_custom_fusion.2
  171.3 1.3 gather_fusion.27
  173.8 2.7 reduce.57
  176.5 1.6 reshape.783
  178.1 7.9 %all-to-all-start.2 = ((bf16[64,2,4096]{2,1,0:T(2,128)(2,1)}), bf16[64,2,4096]{2,1,0:T(2,128)(2,1)S(1)}, u32[]{:S(2)}, u32[]{:S(2)}) async-start(bf16[64,2,4096]{2,1,0:T(2,128)(2,1)} %reshape.783), calls=%async_computation.2 | async-start | bytes 2097152 | tf_op jit(solution)/shard_map/all_to_all | solution.py:117
  190.5 6.2 %maximum_maximum_fusion.2 = bf16[8,9,10,10,64]{4,0,3,2,1:T(8,128)(2,1)} fusion(bf16[8,1,1,1,64]{4,0,3,2,1:T(8,128)(2,1)} %bitcast.602, bf16[8,1,1,8,64]{4,0,3,2,1:T(8,128)(2,1)S(1)} %bitcast.574, bf16[8,1,1,1,64]{4,0,3,2,1:T(8,128)(2,1)} %bitcast.598, bf16[8,1,8,1,64]{4,0,3,2,1:T(8,128)(2,1)S(1)} %bitcast.576, bf16[8,1,8,8,64]{4,0,3,2,1:T(8,128)(2,1)S(1)} %bitcast.545, ...), kind=kLoop, calls=%fused_computation.91 | loop fusion | flops 7833600 | bytes 1843200 | tf_op jit(solution)/shard_map/concatenate | solution.py:37
  196.7 3.3 maximum_maximum_fusion.1
  200.9 11.7 %all-to-all-done.2 = bf16[64,2,4096]{2,1,0:T(2,128)(2,1)S(1)} async-done(((bf16[64,2,4096]{2,1,0:T(2,128)(2,1)}), bf16[64,2,4096]{2,1,0:T(2,128)(2,1)S(1)}, u32[]{:S(2)}, u32[]{:S(2)}) %all-to-all-start.2) | async-done | bytes 1048608 | tf_op jit(solution)/shard_map/all_to_all | solution.py:117
  212.6 3.5 reshape.784
  216.1 2.8 copy.406
  219.6 1.8 convolution_bitcast_fusion.1
  243.8 50.9 %all-reduce.7.cloned.1.call-done = (f32[3,3,3,64,64]{4,3,2,1,0:T(8,128)}, f32[2,2,2,64,128]{4,3,0,1,2:T(8,128)}, f32[128,256]{1,0:T(8,128)}) async-done(((f32[3,3,3,64,64]{4,3,2,1,0:T(8,128)}, f32[2,2,2,64,128]{4,3,0,1,2:T(8,128)}, f32[128,256]{1,0:T(8,128)}), (f32[3,3,3,64,64]{4,3,2,1,0:T(8,128)}, f32[2,2,2,64,128]{4,3,0,1,2:T(8,128)}, f32[128,256]{1,0:T(8,128)})) %all-reduce.7.cloned.1.call-update) | async-done | bytes 835600 | tf_op jit(solution)/shard_map/psum | solution.py:145
  294.6 194.7 %all-reduce.5.cloned.1.call-done = (f32[3,3,3,64,64]{4,3,2,1,0:T(8,128)}, f32[2,2,2,64,128]{4,3,0,1,2:T(8,128)}, f32[128,256]{1,0:T(8,128)}) async-done(((f32[3,3,3,64,64]{4,3,2,1,0:T(8,128)}, f32[2,2,2,64,128]{4,3,0,1,2:T(8,128)}, f32[128,256]{1,0:T(8,128)}), (f32[3,3,3,64,64]{4,3,2,1,0:T(8,128)}, f32[2,2,2,64,128]{4,3,0,1,2:T(8,128)}, f32[128,256]{1,0:T(8,128)})) %all-reduce.5.cloned.1.call-update) | async-done | bytes 835600 | tf_op jit(solution)/shard_map/psum | solution.py:145
  489.4 1.7 copy.325
  491.1 2.2 copy.460
  (243 shorter events, 79.1 us)
Async XLA Ops:
  7.2 102.6 %copy-start = (bf16[3,3,3,64,64]{4,3,2,1,0:T(8,128)(2,1)S(1)}, bf16[3,3,3,64,64]{4,3,2,1,0:T(8,128)(2,1)}, u32[]{:S(2)}) copy-start(bf16[3,3,3,64,64]{4,3,2,1,0:T(8,128)(2,1)} %param.12) | copy-start | bytes 663556
  9.1 33.8 %collective-permute-start = (bf16[8,8,8,8,64]{4,0,3,2,1:T(8,128)(2,1)S(1)}, bf16[8,8,8,8,64]{4,0,3,2,1:T(8,128)(2,1)S(1)}, u32[]{:S(2)}, u32[]{:S(2)}) collective-permute-start(bf16[8,8,8,8,64]{4,0,3,2,1:T(8,128)(2,1)S(1)} %bitcast.503), channel_id=1, source_target_pairs={{0,1},{1,2},{2,3},{3,4},{4,5},{5,6},{6,7},{7,8},{8,9},{9,10},{10,1... | collective-permute-start | bytes 1572872 | tf_op jit(solution)/shard_map/ppermute | solution.py:16
  12.7 30.1 %collective-permute-start.1 = (bf16[8,8,8,8,64]{4,0,3,2,1:T(8,128)(2,1)S(1)}, bf16[8,8,8,8,64]{4,0,3,2,1:T(8,128)(2,1)}, u32[]{:S(2)}, u32[]{:S(2)}) collective-permute-start(bf16[8,8,8,8,64]{4,0,3,2,1:T(8,128)(2,1)S(1)} %bitcast.504), channel_id=1, source_target_pairs={{1,0},{2,1},{3,2},{4,3},{5,4},{6,5},{7,6},{8,7},{9,8},{10,9},{11,1... | collective-permute-start | bytes 1572872 | tf_op jit(solution)/shard_map/ppermute | solution.py:17
  15.3 2.3 copy-start.47
  15.6 2.0 copy-start.50
  17.6 22.8 %all-to-all-start = ((s32[64,1,1]{2,1,0:T(1,128)}), s32[64,1,1]{2,1,0:T(1,128)S(1)}, u32[]{:S(2)}, u32[]{:S(2)}) async-start(s32[64,1,1]{2,1,0:T(1,128)} %copy.303), calls=%async_computation | async-start | bytes 65536 | tf_op jit(solution)/shard_map/all_to_all | solution.py:102
  41.6 4.1 copy-start.48
  58.3 14.6 %copy-start.21 = (bf16[25,8,64]{2,0,1:T(8,128)(2,1)S(1)}, bf16[25,8,64]{2,0,1:T(8,128)(2,1)}, u32[]{:S(2)}) copy-start(bf16[25,8,64]{2,0,1:T(8,128)(2,1)} %get-tuple-element.50) | copy-start | bytes 76804
  64.9 44.9 %copy-start.6 = (bf16[8,8,8,64]{3,0,2,1:T(8,128)(2,1)}, bf16[8,8,8,64]{3,0,2,1:T(8,128)(2,1)S(1)}, u32[]{:S(2)}) copy-start(bf16[8,8,8,64]{3,0,2,1:T(8,128)(2,1)S(1)} %copy.409) | copy-start | bytes 196612
  78.7 20.0 %copy-start.1 = (bf16[8,8,8,8,64]{4,3,2,1,0:T(8,128)(2,1)}, bf16[8,8,8,8,64]{4,3,2,1,0:T(8,128)(2,1)S(1)}, u32[]{:S(2)}) copy-start(bf16[8,8,8,8,64]{4,3,2,1,0:T(8,128)(2,1)S(1)} %gather_fusion.13) | copy-start | bytes 1572868
  95.9 20.7 %copy-start.32 = (bf16[8,8,64]{2,0,1:T(8,128)(2,1)}, bf16[8,8,64]{2,0,1:T(8,128)(2,1)S(1)}, u32[]{:S(2)}) copy-start(bf16[8,8,64]{2,0,1:T(8,128)(2,1)S(1)} %copy.425) | copy-start | bytes 24580
  98.6 18.0 %copy-start.14 = (bf16[8,8,8,64]{3,0,2,1:T(8,128)(2,1)}, bf16[8,8,8,64]{3,0,2,1:T(8,128)(2,1)S(1)}, u32[]{:S(2)}) copy-start(bf16[8,8,8,64]{3,0,2,1:T(8,128)(2,1)S(1)} %copy.413) | copy-start | bytes 196612
  100.1 16.6 %copy-start.35 = (bf16[8,64]{1,0:T(8,128)(2,1)}, bf16[8,64]{1,0:T(8,128)(2,1)S(1)}, u32[]{:S(2)}) copy-start(bf16[8,64]{1,0:T(8,128)(2,1)S(1)} %gather_fusion.8) | copy-start | bytes 3076
  101.4 15.2 %copy-start.37 = (bf16[8,64]{1,0:T(8,128)(2,1)}, bf16[8,64]{1,0:T(8,128)(2,1)S(1)}, u32[]{:S(2)}) copy-start(bf16[8,64]{1,0:T(8,128)(2,1)S(1)} %gather_fusion.18) | copy-start | bytes 3076
  102.8 13.8 %copy-start.38 = (bf16[8,64]{1,0:T(8,128)(2,1)}, bf16[8,64]{1,0:T(8,128)(2,1)S(1)}, u32[]{:S(2)}) copy-start(bf16[8,64]{1,0:T(8,128)(2,1)S(1)} %gather_fusion.20) | copy-start | bytes 3076
  104.2 12.4 %copy-start.41 = (bf16[8,64]{1,0:T(8,128)(2,1)}, bf16[8,64]{1,0:T(8,128)(2,1)S(1)}, u32[]{:S(2)}) copy-start(bf16[8,64]{1,0:T(8,128)(2,1)S(1)} %gather_fusion.24) | copy-start | bytes 3076
  105.6 11.0 %copy-start.44 = (bf16[8,64]{1,0:T(8,128)(2,1)}, bf16[8,64]{1,0:T(8,128)(2,1)S(1)}, u32[]{:S(2)}) copy-start(bf16[8,64]{1,0:T(8,128)(2,1)S(1)} %gather_fusion.26) | copy-start | bytes 3076
  107.0 9.6 %copy-start.39 = (bf16[8,64]{1,0:T(8,128)(2,1)}, bf16[8,64]{1,0:T(8,128)(2,1)S(1)}, u32[]{:S(2)}) copy-start(bf16[8,64]{1,0:T(8,128)(2,1)S(1)} %gather_fusion.6) | copy-start | bytes 3076
  108.4 8.3 %copy-start.42 = (bf16[8,64]{1,0:T(8,128)(2,1)}, bf16[8,64]{1,0:T(8,128)(2,1)S(1)}, u32[]{:S(2)}) copy-start(bf16[8,64]{1,0:T(8,128)(2,1)S(1)} %gather_fusion.2) | copy-start | bytes 3076
  109.8 6.9 %copy-start.45 = (bf16[8,64]{1,0:T(8,128)(2,1)}, bf16[8,64]{1,0:T(8,128)(2,1)S(1)}, u32[]{:S(2)}) copy-start(bf16[8,64]{1,0:T(8,128)(2,1)S(1)} %gather_fusion) | copy-start | bytes 3076
  109.8 6.9 %copy-start.24 = (bf16[2,2,2,64,128]{4,3,2,1,0:T(8,128)(2,1)S(1)}, bf16[2,2,2,64,128]{4,3,2,1,0:T(8,128)(2,1)}, u32[]{:S(2)}) copy-start(bf16[2,2,2,64,128]{4,3,2,1,0:T(8,128)(2,1)} %param.13) | copy-start | bytes 393220
  121.9 12.9 %copy-start.49 = (s32[64]{0:T(128)S(1)}, s32[64]{0:T(128)}, u32[]{:S(2)}) copy-start(s32[64]{0:T(128)} %copy-done.48) | copy-start | bytes 772
  124.5 36.9 %all-to-all-start.1 = ((bf16[64,2,4096]{2,1,0:T(2,128)(2,1)}), bf16[64,2,4096]{2,1,0:T(2,128)(2,1)S(1)}, u32[]{:S(2)}, u32[]{:S(2)}) async-start(bf16[64,2,4096]{2,1,0:T(2,128)(2,1)} %reshape.781), calls=%async_computation.1 | async-start | bytes 2097152 | tf_op jit(solution)/shard_map/all_to_all | solution.py:110
  134.9 34.8 %copy-start.34 = (bf16[128,256]{1,0:T(8,128)(2,1)S(1)}, bf16[128,256]{1,0:T(8,128)(2,1)}, u32[]{:S(2)}) copy-start(bf16[128,256]{1,0:T(8,128)(2,1)} %param.14) | copy-start | bytes 196612
  176.4 14.0 %copy-start.7 = (bf16[8,8,8,64]{3,0,2,1:T(8,128)(2,1)S(1)}, bf16[8,8,8,64]{3,0,2,1:T(8,128)(2,1)}, u32[]{:S(2)}) copy-start(bf16[8,8,8,64]{3,0,2,1:T(8,128)(2,1)} %copy-done.6) | copy-start | bytes 196612
  176.5 14.0 %copy-start.8 = (bf16[8,8,8,64]{3,0,2,1:T(8,128)(2,1)S(1)}, bf16[8,8,8,64]{3,0,2,1:T(8,128)(2,1)}, u32[]{:S(2)}) copy-start(bf16[8,8,8,64]{3,0,2,1:T(8,128)(2,1)} %copy.412) | copy-start | bytes 196612
  176.5 14.0 %copy-start.13 = (bf16[8,8,8,64]{3,0,2,1:T(8,128)(2,1)S(1)}, bf16[8,8,8,64]{3,0,2,1:T(8,128)(2,1)}, u32[]{:S(2)}) copy-start(bf16[8,8,8,64]{3,0,2,1:T(8,128)(2,1)} %copy.408) | copy-start | bytes 196612
  176.5 13.9 %copy-start.22 = (bf16[8,8,64]{2,0,1:T(8,128)(2,1)S(1)}, bf16[8,8,64]{2,0,1:T(8,128)(2,1)}, u32[]{:S(2)}) copy-start(bf16[8,8,64]{2,0,1:T(8,128)(2,1)} %copy.420) | copy-start | bytes 24580
  176.5 13.9 %copy-start.23 = (bf16[8,8,64]{2,0,1:T(8,128)(2,1)S(1)}, bf16[8,8,64]{2,0,1:T(8,128)(2,1)}, u32[]{:S(2)}) copy-start(bf16[8,8,64]{2,0,1:T(8,128)(2,1)} %copy.421) | copy-start | bytes 24580
  176.5 13.9 %copy-start.27 = (bf16[8,8,64]{2,0,1:T(8,128)(2,1)S(1)}, bf16[8,8,64]{2,0,1:T(8,128)(2,1)}, u32[]{:S(2)}) copy-start(bf16[8,8,64]{2,0,1:T(8,128)(2,1)} %copy.414) | copy-start | bytes 24580
  176.5 13.9 %copy-start.28 = (bf16[8,8,64]{2,0,1:T(8,128)(2,1)S(1)}, bf16[8,8,64]{2,0,1:T(8,128)(2,1)}, u32[]{:S(2)}) copy-start(bf16[8,8,64]{2,0,1:T(8,128)(2,1)} %copy.415) | copy-start | bytes 24580
  178.1 34.5 %all-to-all-start.2 = ((bf16[64,2,4096]{2,1,0:T(2,128)(2,1)}), bf16[64,2,4096]{2,1,0:T(2,128)(2,1)S(1)}, u32[]{:S(2)}, u32[]{:S(2)}) async-start(bf16[64,2,4096]{2,1,0:T(2,128)(2,1)} %reshape.783), calls=%async_computation.2 | async-start | bytes 2097152 | tf_op jit(solution)/shard_map/all_to_all | solution.py:117
  186.0 108.6 %all-reduce.7.cloned.1.call-start = ((), (), s32[]{:S(2)}) async-start(), calls=%async_computation.4 | async-start | bytes 2555904 | tf_op jit(solution)/shard_map/psum | solution.py:145
  189.4 7.2 %copy-start.15 = (bf16[8,8,8,64]{3,0,2,1:T(8,128)(2,1)S(1)}, bf16[8,8,8,64]{3,0,2,1:T(8,128)(2,1)}, u32[]{:S(2)}) copy-start(bf16[8,8,8,64]{3,0,2,1:T(8,128)(2,1)} %copy-done.14) | copy-start | bytes 196612
  189.4 7.2 %copy-start.29 = (bf16[8,8,64]{2,0,1:T(8,128)(2,1)S(1)}, bf16[8,8,64]{2,0,1:T(8,128)(2,1)}, u32[]{:S(2)}) copy-start(bf16[8,8,64]{2,0,1:T(8,128)(2,1)} %copy.422) | copy-start | bytes 24580
  189.4 7.2 %copy-start.30 = (bf16[8,8,64]{2,0,1:T(8,128)(2,1)S(1)}, bf16[8,8,64]{2,0,1:T(8,128)(2,1)}, u32[]{:S(2)}) copy-start(bf16[8,8,64]{2,0,1:T(8,128)(2,1)} %copy.423) | copy-start | bytes 24580
  189.4 7.2 %copy-start.31 = (bf16[8,8,64]{2,0,1:T(8,128)(2,1)S(1)}, bf16[8,8,64]{2,0,1:T(8,128)(2,1)}, u32[]{:S(2)}) copy-start(bf16[8,8,64]{2,0,1:T(8,128)(2,1)} %copy.424) | copy-start | bytes 24580
  189.5 7.2 %copy-start.33 = (bf16[8,8,64]{2,0,1:T(8,128)(2,1)S(1)}, bf16[8,8,64]{2,0,1:T(8,128)(2,1)}, u32[]{:S(2)}) copy-start(bf16[8,8,64]{2,0,1:T(8,128)(2,1)} %copy-done.32) | copy-start | bytes 24580
  189.5 7.2 %copy-start.36 = (bf16[8,64]{1,0:T(8,128)(2,1)S(1)}, bf16[8,64]{1,0:T(8,128)(2,1)}, u32[]{:S(2)}) copy-start(bf16[8,64]{1,0:T(8,128)(2,1)} %copy-done.35) | copy-start | bytes 3076
  189.5 7.2 %copy-start.40 = (bf16[8,64]{1,0:T(8,128)(2,1)S(1)}, bf16[8,64]{1,0:T(8,128)(2,1)}, u32[]{:S(2)}) copy-start(bf16[8,64]{1,0:T(8,128)(2,1)} %copy-done.39) | copy-start | bytes 3076
  189.5 7.2 %copy-start.43 = (bf16[8,64]{1,0:T(8,128)(2,1)S(1)}, bf16[8,64]{1,0:T(8,128)(2,1)}, u32[]{:S(2)}) copy-start(bf16[8,64]{1,0:T(8,128)(2,1)} %copy-done.42) | copy-start | bytes 3076
  189.5 7.2 %copy-start.46 = (bf16[8,64]{1,0:T(8,128)(2,1)S(1)}, bf16[8,64]{1,0:T(8,128)(2,1)}, u32[]{:S(2)}) copy-start(bf16[8,64]{1,0:T(8,128)(2,1)} %copy-done.45) | copy-start | bytes 3076
  196.7 3.3 copy-start.17
  216.1 3.5 copy-start.10
  216.1 3.5 copy-start.52
  219.6 1.8 copy-start.25
  243.7 245.7 %all-reduce.5.cloned.1.call-start = ((), (), s32[]{:S(2)}) async-start(), calls=%async_computation.3 | async-start | bytes 2555904 | tf_op jit(solution)/shard_map/psum | solution.py:145
  489.4 3.9 copy-start.26
  (13 other events, 15.5 us)
Sparse Core Ops, SparseCore 0:
  243.8 50.7 all-reduce.6
  298.3 191.0 all-reduce.4
